TPU v7x, 32 devices: a whole 2x2x4 slice. The times are simulated.
32 devices in a mesh: batch: 4 (over z), seq: 8 (over y, x, core).
Axes of the slice: x: 2, y: 2, z: 4, core: 2. Of those that a mesh axis runs over, the one named last changes fastest.
Arguments:
- queries: bfloat16 [16384, 8, 256], P(('batch', 'seq')), parts along dimension 0, may hold values from -400 to 400
- key_heads: bfloat16 [16384, 4, 256], P(('batch', 'seq')), parts along dimension 0, may hold values from -16 to 16
- projected_value_heads: bfloat16 [16384, 4, 256], P(('batch', 'seq')), parts along dimension 0, may hold values from -6 to 6
- lengths: int32 [4], P('batch'), parts along dimension 0, may hold values from 3585 to 4096
Outputs:
- attended: bfloat16 [16384, 8, 256], P(('batch', 'seq')), parts along dimension 0
There are 4 independent parts, one for each index of `batch`. A program takes and returns all parts, laid end to end along the dimension named above; each array names one. Nothing has to cross between parts.
All inputs are finite; a program needn't handle non-finite values.
Results may differ from a plain program's by a relative error of at most 0.0033.
Values may be sent and summed in bfloat16 or wider, within the bound.
No kernel may reach another device: no remote copies, remote signals or barrier semaphores. Data moves between devices by JAX's collectives and lax.ppermute only.
A program may use at most 192 MiB of HBM per device.

v0:
```python
import math
import jax
import jax.numpy as jnp
from jax import lax
from jax.sharding import PartitionSpec as P

WINDOW = 4096
SINKS = 4


def spread(value, axis, source):
    kept = jnp.where(lax.axis_index(axis) == source, value, 0).astype(value.dtype)
    return lax.psum(kept, axis)


def shards(queries, key_heads, projected_value_heads, lengths):
    tok_rows = queries.shape[0]
    head_count = queries.shape[1]
    head_width = queries.shape[2]
    kv_heads = key_heads.shape[1]
    share = head_count // kv_heads
    position = lax.axis_index("seq")
    length_now = lengths[0]
    first_row = position * tok_rows
    score_scale = head_width ** (-0.5)
    grouped = queries.reshape(tok_rows, kv_heads, share, head_width)
    query_pos = first_row + jnp.arange(tok_rows, dtype=jnp.int32)
    last_query = first_row + tok_rows - 1

    def attend(running, kv_block, key_start, sink_mode):
        key_count = kv_block.shape[1]
        key_pos = key_start + jnp.arange(key_count, dtype=jnp.int32)
        if sink_mode:
            useful = first_row < length_now
        else:
            useful = (
                (key_start <= last_query)
                & (key_start + key_count - 1 > first_row - WINDOW)
                & (key_start < length_now)
                & (first_row < length_now)
                & (key_start + key_count > SINKS)
            )

        def compute(current):
            maximum, totals, weighted = current
            scores = (
                jnp.einsum(
                    "qhgd,khd->hgqk", grouped, kv_block[0], preferred_element_type=jnp.float32
                )
                * score_scale
            )
            distance = query_pos[:, None] - key_pos[None, :]
            if sink_mode:
                visible = (distance >= 0) & (key_pos[None, :] < length_now)
            else:
                visible = (
                    (distance >= 0)
                    & (distance < WINDOW)
                    & (key_pos[None, :] >= SINKS)
                    & (key_pos[None, :] < length_now)
                )
            visible = visible & (query_pos[:, None] < length_now)
            masked = jnp.where(visible, scores, -1e30)
            newest = jnp.maximum(maximum, jnp.max(masked, axis=-1))
            weights = jnp.where(visible, jnp.exp(scores - newest[..., None]), 0.0)
            rescale = jnp.exp(maximum - newest)
            totals = totals * rescale + jnp.sum(weights, axis=-1)
            weighted = weighted * rescale[..., None] + jnp.einsum(
                "hgqk,khd->hgqd",
                weights.astype(jnp.bfloat16),
                kv_block[1],
                preferred_element_type=jnp.float32,
            )
            return (newest, totals, weighted)

        return lax.cond(useful, compute, lambda current: current, running)

    running = (
        jnp.full((kv_heads, share, tok_rows), -1e30, jnp.float32),
        jnp.zeros((kv_heads, share, tok_rows), jnp.float32),
        jnp.zeros((kv_heads, share, tok_rows, head_width), jnp.float32),
    )
    own_pair = jnp.stack([key_heads, projected_value_heads])
    sink_pair = spread(own_pair[:, :SINKS], "seq", 0)
    running = attend(running, sink_pair, jnp.int32(0), True)
    shard_piece = lax.all_gather(own_pair, "seq", axis=1, tiled=True)
    piece_rows = shard_piece.shape[1]
    block_size = math.gcd(piece_rows, tok_rows)

    def one_slice(slice_index, inner):
        sliced = lax.dynamic_slice_in_dim(shard_piece, slice_index * block_size, block_size, 1)
        return attend(inner, sliced, slice_index * block_size, False)

    running = lax.fori_loop(0, piece_rows // block_size, one_slice, running)
    maximum, totals, weighted = running
    valid = query_pos < length_now
    result = jnp.where(valid[:, None], weighted / jnp.where(valid, totals, 1.0)[..., None], 0.0)
    return (
        result.transpose(2, 0, 1, 3).reshape(tok_rows, head_count, head_width).astype(jnp.bfloat16)
    )


def solution(mesh):
    in_specs = (
        P(("batch", "seq"), None, None),
        P(("batch", "seq"), None, None),
        P(("batch", "seq"), None, None),
        P("batch"),
    )
    out_specs = P(("batch", "seq"), None, None)
    return jax.shard_map(shards, mesh=mesh, in_specs=in_specs, out_specs=out_specs, check_vma=False)
```

profile of v0, /device:TPU:7, one launch (start us, length us, event | category | flops | bytes accessed | tf_op | source)
XLA Modules:
  0.0 233.9 jit_solution(17987228410753566416)
XLA Ops:
  6.5 1.8 copy_bitcast_fusion
  8.4 1.5 pad_maximum_fusion
  10.5 3.3 %copy.8 = bf16[512,8,256]{2,0,1:T(8,128)(2,1)} copy(bf16[512,8,256]{2,1,0:T(8,128)(2,1)} %param.10) | data formatting | bytes 4194304 | tf_op args[0]
  13.9 23.0 %psum.7 = bf16[2,4,4,256]{3,1,2,0:T(4,128)(2,1)S(1)} all-reduce(bf16[2,4,4,256]{3,1,2,0:T(4,128)(2,1)S(1)} %fusion.40), channel_id=1, replica_groups=mesh['batch'=4,'seq'=8] {'seq'}, use_global_device_ids=true, to_apply=%region_0.1 | all-reduce | flops 8192 | bytes 32768 | tf_op jit(solution)/shard_map/psum | solution.py:13
  36.9 9.0 %conditional.2 = (f32[4,2,512]{2,1,0:T(2,128)}, f32[4,2,512]{2,1,0:T(2,128)S(1)}, f32[4,2,512,256]{3,2,1,0:T(8,128)}) conditional(s32[]{:T(128)} %convert_element_type.35, () %tuple.61, (s32[512]{0:T(512)S(1)}, s32[4]{0:T(128)S(1)}, s32[]{:T(128)}, s32[4]{0:T(128)S(1)}, bf16[2,4,4,256]{3,1,2,0:T(4,128)(2,1)S(1)}, ...), branch_computations={%region_1.2_spmd, %region_2.5_spmd} | conditional | flops 17998340 | bytes 6698056 | solution.py:76
  38.3 2.3 select_reduce_fusion
  41.2 0.8 fusion.4
  42.0 0.7 fusion.16
  42.8 3.2 %convolution_add_fusion = f32[4,2,512,256]{3,2,1,0:T(8,128)} fusion(f32[4,2,512]{2,1,0:T(2,128)S(1)} %get-tuple-element.538, f32[4,2,512,4]{2,3,1,0:T(4,128)S(1)} %get-tuple-element.547, f32[4,2,512]{2,1,0:T(2,128)} %get-tuple-element.637, pred[512,4]{0,1:T(4,128)(4,1)S(1)} %fusion.14, bf16[2,4,4,256]{3,1,2,0:T(4,128)(2,1)S(1)} %get-tuple-element.449), kind=kOutput, calls=%fused_computation.1 | convolution fusion | flops 9486336 | bytes 4302848 | tf_op jit(solution)/shard_map/cond/branch_1_fun/hgqk,khd->hgqd/dot_general | solution.py:68
  46.0 54.7 %all-gather.2.cloned.1.call-done = bf16[2,4096,4,256]{3,1,2,0:T(8,128)(2,1)} async-done(((bf16[2,512,4,256]{3,1,2,0:T(8,128)(2,1)}), bf16[2,4096,4,256]{3,1,2,0:T(8,128)(2,1)}) %all-gather.2.cloned.1.call-update) | async-done | bytes 16777232 | tf_op jit(solution)/shard_map/all_gather | solution.py:86
  100.6 121.3 %while.22 = (s32[]{:T(128)}, f32[4,2,512]{2,1,0:T(2,128)}, f32[4,2,512]{2,1,0:T(2,128)S(1)}, f32[4,2,512,256]{3,2,1,0:T(8,128)}, s32[]{:T(128)}, /*index=5*/s32[...) while((s32[]{:T(128)}, f32[4,2,512]{2,1,0:T(2,128)}, ...), condition=%wide.region_10.11_spmd.clone, body=%wide.region_5.10_spmd.clone.sunk | while | flops 2174495232 | bytes 39079348 | solution.py:94
  101.3 14.5 %conditional.5 = ((f32[4,2,512]{2,1,0:T(2,128)}, f32[4,2,512]{2,1,0:T(2,128)S(1)}, f32[4,2,512,256]{3,2,1,0:T(8,128)})) conditional(s32[]{:T(128)} %convert_element_type.48, (f32[4,2,512]{2,1,0:T(2,128)}, f32[4,2,512]{2,1,0:T(2,128)S(1)}, f32[4,2,512,256]{3,2,1,0:T(8,128)}) %tuple.88, (s32[]{:T(128)}, s32[]{:T(128)}, s32[512]{0:T(512)S(1)}, ...), branch_computations={%region_6.6_spmd, %region_7.9_spmd} | conditional | flops 2174495232 | bytes 39076968 | solution.py:76
  102.4 3.5 %fusion.17 = (f32[4,2,512]{2,1,0:T(2,128)S(1)}, f32[4,512,512,2]{2,1,3,0:T(8,128)S(1)}) fusion(pred[512,512]{0,1:T(8,128)(4,1)S(1)} %fusion.34, bf16[512,4,2,256]{3,0,2,1:T(8,128)(2,1)} %get-tuple-element.457, bf16[2,4096,4,256]{3,1,2,0:T(8,128)(2,1)} %get-tuple-element.456, s32[]{:T(128)S(6)} %select_n.38), kind=kOutput, calls=%fused_computation.26 | convolution fusion | flops 1080029184 | bytes 11812868 | tf_op jit(solution)/shard_map/while/body/eval_jaxpr/cond/branch_1_fun/qhgd,khd->hgqk/dot_general | solution.py:47
  106.6 1.7 fusion.21
  109.1 6.1 %multiply_add_fusion = f32[4,2,512,256]{3,2,1,0:T(8,128)} fusion(f32[4,2,512,256]{3,2,1,0:T(8,128)} %get-tuple-element.459, f32[4,2,512]{2,1,0:T(2,128)S(1)} %bitcast.69, f32[4,512,512,2]{2,1,3,0:T(8,128)S(1)} %get-tuple-element.549, f32[4,2,512]{2,1,0:T(2,128)S(1)} %max.4, pred[512,512]{0,1:T(8,128)(4,1)S(1)} %fusion.34, ...), kind=kOutput, calls=%fused_computation.32 | convolution fusion | flops 1084227584 | bytes 18120712 | tf_op jit(solution)/shard_map/while/body/eval_jaxpr/cond/branch_1_fun/hgqk,khd->hgqd/dot_general | solution.py:68
  116.4 14.5 %conditional.5 = ((f32[4,2,512]{2,1,0:T(2,128)}, f32[4,2,512]{2,1,0:T(2,128)S(1)}, f32[4,2,512,256]{3,2,1,0:T(8,128)})) conditional(s32[]{:T(128)} %convert_element_type.48, (f32[4,2,512]{2,1,0:T(2,128)}, f32[4,2,512]{2,1,0:T(2,128)S(1)}, f32[4,2,512,256]{3,2,1,0:T(8,128)}) %tuple.88, (s32[]{:T(128)}, s32[]{:T(128)}, s32[512]{0:T(512)S(1)}, ...), branch_computations={%region_6.6_spmd, %region_7.9_spmd} | conditional | flops 2174495232 | bytes 39076968 | solution.py:76
  117.6 3.5 %fusion.17 = (f32[4,2,512]{2,1,0:T(2,128)S(1)}, f32[4,512,512,2]{2,1,3,0:T(8,128)S(1)}) fusion(pred[512,512]{0,1:T(8,128)(4,1)S(1)} %fusion.34, bf16[512,4,2,256]{3,0,2,1:T(8,128)(2,1)} %get-tuple-element.457, bf16[2,4096,4,256]{3,1,2,0:T(8,128)(2,1)} %get-tuple-element.456, s32[]{:T(128)S(6)} %select_n.38), kind=kOutput, calls=%fused_computation.26 | convolution fusion | flops 1080029184 | bytes 11812868 | tf_op jit(solution)/shard_map/while/body/eval_jaxpr/cond/branch_1_fun/qhgd,khd->hgqk/dot_general | solution.py:47
  121.0 0.7 max.4
  121.8 1.7 fusion.21
  124.2 6.1 %multiply_add_fusion = f32[4,2,512,256]{3,2,1,0:T(8,128)} fusion(f32[4,2,512,256]{3,2,1,0:T(8,128)} %get-tuple-element.459, f32[4,2,512]{2,1,0:T(2,128)S(1)} %bitcast.69, f32[4,512,512,2]{2,1,3,0:T(8,128)S(1)} %get-tuple-element.549, f32[4,2,512]{2,1,0:T(2,128)S(1)} %max.4, pred[512,512]{0,1:T(8,128)(4,1)S(1)} %fusion.34, ...), kind=kOutput, calls=%fused_computation.32 | convolution fusion | flops 1084227584 | bytes 18120712 | tf_op jit(solution)/shard_map/while/body/eval_jaxpr/cond/branch_1_fun/hgqk,khd->hgqd/dot_general | solution.py:68
  131.6 14.5 %conditional.5 = ((f32[4,2,512]{2,1,0:T(2,128)}, f32[4,2,512]{2,1,0:T(2,128)S(1)}, f32[4,2,512,256]{3,2,1,0:T(8,128)})) conditional(s32[]{:T(128)} %convert_element_type.48, (f32[4,2,512]{2,1,0:T(2,128)}, f32[4,2,512]{2,1,0:T(2,128)S(1)}, f32[4,2,512,256]{3,2,1,0:T(8,128)}) %tuple.88, (s32[]{:T(128)}, s32[]{:T(128)}, s32[512]{0:T(512)S(1)}, ...), branch_computations={%region_6.6_spmd, %region_7.9_spmd} | conditional | flops 2174495232 | bytes 39076968 | solution.py:76
  132.7 3.5 %fusion.17 = (f32[4,2,512]{2,1,0:T(2,128)S(1)}, f32[4,512,512,2]{2,1,3,0:T(8,128)S(1)}) fusion(pred[512,512]{0,1:T(8,128)(4,1)S(1)} %fusion.34, bf16[512,4,2,256]{3,0,2,1:T(8,128)(2,1)} %get-tuple-element.457, bf16[2,4096,4,256]{3,1,2,0:T(8,128)(2,1)} %get-tuple-element.456, s32[]{:T(128)S(6)} %select_n.38), kind=kOutput, calls=%fused_computation.26 | convolution fusion | flops 1080029184 | bytes 11812868 | tf_op jit(solution)/shard_map/while/body/eval_jaxpr/cond/branch_1_fun/qhgd,khd->hgqk/dot_general | solution.py:47
  136.2 0.7 max.4
  136.9 1.7 fusion.21
  139.4 6.1 %multiply_add_fusion = f32[4,2,512,256]{3,2,1,0:T(8,128)} fusion(f32[4,2,512,256]{3,2,1,0:T(8,128)} %get-tuple-element.459, f32[4,2,512]{2,1,0:T(2,128)S(1)} %bitcast.69, f32[4,512,512,2]{2,1,3,0:T(8,128)S(1)} %get-tuple-element.549, f32[4,2,512]{2,1,0:T(2,128)S(1)} %max.4, pred[512,512]{0,1:T(8,128)(4,1)S(1)} %fusion.34, ...), kind=kOutput, calls=%fused_computation.32 | convolution fusion | flops 1084227584 | bytes 18120712 | tf_op jit(solution)/shard_map/while/body/eval_jaxpr/cond/branch_1_fun/hgqk,khd->hgqd/dot_general | solution.py:68
  146.8 14.5 %conditional.5 = ((f32[4,2,512]{2,1,0:T(2,128)}, f32[4,2,512]{2,1,0:T(2,128)S(1)}, f32[4,2,512,256]{3,2,1,0:T(8,128)})) conditional(s32[]{:T(128)} %convert_element_type.48, (f32[4,2,512]{2,1,0:T(2,128)}, f32[4,2,512]{2,1,0:T(2,128)S(1)}, f32[4,2,512,256]{3,2,1,0:T(8,128)}) %tuple.88, (s32[]{:T(128)}, s32[]{:T(128)}, s32[512]{0:T(512)S(1)}, ...), branch_computations={%region_6.6_spmd, %region_7.9_spmd} | conditional | flops 2174495232 | bytes 39076968 | solution.py:76
  147.9 3.5 %fusion.17 = (f32[4,2,512]{2,1,0:T(2,128)S(1)}, f32[4,512,512,2]{2,1,3,0:T(8,128)S(1)}) fusion(pred[512,512]{0,1:T(8,128)(4,1)S(1)} %fusion.34, bf16[512,4,2,256]{3,0,2,1:T(8,128)(2,1)} %get-tuple-element.457, bf16[2,4096,4,256]{3,1,2,0:T(8,128)(2,1)} %get-tuple-element.456, s32[]{:T(128)S(6)} %select_n.38), kind=kOutput, calls=%fused_computation.26 | convolution fusion | flops 1080029184 | bytes 11812868 | tf_op jit(solution)/shard_map/while/body/eval_jaxpr/cond/branch_1_fun/qhgd,khd->hgqk/dot_general | solution.py:47
  152.1 1.7 fusion.21
  154.6 6.1 %multiply_add_fusion = f32[4,2,512,256]{3,2,1,0:T(8,128)} fusion(f32[4,2,512,256]{3,2,1,0:T(8,128)} %get-tuple-element.459, f32[4,2,512]{2,1,0:T(2,128)S(1)} %bitcast.69, f32[4,512,512,2]{2,1,3,0:T(8,128)S(1)} %get-tuple-element.549, f32[4,2,512]{2,1,0:T(2,128)S(1)} %max.4, pred[512,512]{0,1:T(8,128)(4,1)S(1)} %fusion.34, ...), kind=kOutput, calls=%fused_computation.32 | convolution fusion | flops 1084227584 | bytes 18120712 | tf_op jit(solution)/shard_map/while/body/eval_jaxpr/cond/branch_1_fun/hgqk,khd->hgqd/dot_general | solution.py:68
  161.9 14.5 %conditional.5 = ((f32[4,2,512]{2,1,0:T(2,128)}, f32[4,2,512]{2,1,0:T(2,128)S(1)}, f32[4,2,512,256]{3,2,1,0:T(8,128)})) conditional(s32[]{:T(128)} %convert_element_type.48, (f32[4,2,512]{2,1,0:T(2,128)}, f32[4,2,512]{2,1,0:T(2,128)S(1)}, f32[4,2,512,256]{3,2,1,0:T(8,128)}) %tuple.88, (s32[]{:T(128)}, s32[]{:T(128)}, s32[512]{0:T(512)S(1)}, ...), branch_computations={%region_6.6_spmd, %region_7.9_spmd} | conditional | flops 2174495232 | bytes 39076968 | solution.py:76
  163.0 3.5 %fusion.17 = (f32[4,2,512]{2,1,0:T(2,128)S(1)}, f32[4,512,512,2]{2,1,3,0:T(8,128)S(1)}) fusion(pred[512,512]{0,1:T(8,128)(4,1)S(1)} %fusion.34, bf16[512,4,2,256]{3,0,2,1:T(8,128)(2,1)} %get-tuple-element.457, bf16[2,4096,4,256]{3,1,2,0:T(8,128)(2,1)} %get-tuple-element.456, s32[]{:T(128)S(6)} %select_n.38), kind=kOutput, calls=%fused_computation.26 | convolution fusion | flops 1080029184 | bytes 11812868 | tf_op jit(solution)/shard_map/while/body/eval_jaxpr/cond/branch_1_fun/qhgd,khd->hgqk/dot_general | solution.py:47
  167.2 1.7 fusion.21
  169.7 6.1 %multiply_add_fusion = f32[4,2,512,256]{3,2,1,0:T(8,128)} fusion(f32[4,2,512,256]{3,2,1,0:T(8,128)} %get-tuple-element.459, f32[4,2,512]{2,1,0:T(2,128)S(1)} %bitcast.69, f32[4,512,512,2]{2,1,3,0:T(8,128)S(1)} %get-tuple-element.549, f32[4,2,512]{2,1,0:T(2,128)S(1)} %max.4, pred[512,512]{0,1:T(8,128)(4,1)S(1)} %fusion.34, ...), kind=kOutput, calls=%fused_computation.32 | convolution fusion | flops 1084227584 | bytes 18120712 | tf_op jit(solution)/shard_map/while/body/eval_jaxpr/cond/branch_1_fun/hgqk,khd->hgqd/dot_general | solution.py:68
  177.1 14.5 %conditional.5 = ((f32[4,2,512]{2,1,0:T(2,128)}, f32[4,2,512]{2,1,0:T(2,128)S(1)}, f32[4,2,512,256]{3,2,1,0:T(8,128)})) conditional(s32[]{:T(128)} %convert_element_type.48, (f32[4,2,512]{2,1,0:T(2,128)}, f32[4,2,512]{2,1,0:T(2,128)S(1)}, f32[4,2,512,256]{3,2,1,0:T(8,128)}) %tuple.88, (s32[]{:T(128)}, s32[]{:T(128)}, s32[512]{0:T(512)S(1)}, ...), branch_computations={%region_6.6_spmd, %region_7.9_spmd} | conditional | flops 2174495232 | bytes 39076968 | solution.py:76
  178.2 3.5 %fusion.17 = (f32[4,2,512]{2,1,0:T(2,128)S(1)}, f32[4,512,512,2]{2,1,3,0:T(8,128)S(1)}) fusion(pred[512,512]{0,1:T(8,128)(4,1)S(1)} %fusion.34, bf16[512,4,2,256]{3,0,2,1:T(8,128)(2,1)} %get-tuple-element.457, bf16[2,4096,4,256]{3,1,2,0:T(8,128)(2,1)} %get-tuple-element.456, s32[]{:T(128)S(6)} %select_n.38), kind=kOutput, calls=%fused_computation.26 | convolution fusion | flops 1080029184 | bytes 11812868 | tf_op jit(solution)/shard_map/while/body/eval_jaxpr/cond/branch_1_fun/qhgd,khd->hgqk/dot_general | solution.py:47
  181.7 0.7 max.4
  182.4 1.7 fusion.21
  184.9 6.1 %multiply_add_fusion = f32[4,2,512,256]{3,2,1,0:T(8,128)} fusion(f32[4,2,512,256]{3,2,1,0:T(8,128)} %get-tuple-element.459, f32[4,2,512]{2,1,0:T(2,128)S(1)} %bitcast.69, f32[4,512,512,2]{2,1,3,0:T(8,128)S(1)} %get-tuple-element.549, f32[4,2,512]{2,1,0:T(2,128)S(1)} %max.4, pred[512,512]{0,1:T(8,128)(4,1)S(1)} %fusion.34, ...), kind=kOutput, calls=%fused_computation.32 | convolution fusion | flops 1084227584 | bytes 18120712 | tf_op jit(solution)/shard_map/while/body/eval_jaxpr/cond/branch_1_fun/hgqk,khd->hgqd/dot_general | solution.py:68
  192.2 14.5 %conditional.5 = ((f32[4,2,512]{2,1,0:T(2,128)}, f32[4,2,512]{2,1,0:T(2,128)S(1)}, f32[4,2,512,256]{3,2,1,0:T(8,128)})) conditional(s32[]{:T(128)} %convert_element_type.48, (f32[4,2,512]{2,1,0:T(2,128)}, f32[4,2,512]{2,1,0:T(2,128)S(1)}, f32[4,2,512,256]{3,2,1,0:T(8,128)}) %tuple.88, (s32[]{:T(128)}, s32[]{:T(128)}, s32[512]{0:T(512)S(1)}, ...), branch_computations={%region_6.6_spmd, %region_7.9_spmd} | conditional | flops 2174495232 | bytes 39076968 | solution.py:76
  193.4 3.5 %fusion.17 = (f32[4,2,512]{2,1,0:T(2,128)S(1)}, f32[4,512,512,2]{2,1,3,0:T(8,128)S(1)}) fusion(pred[512,512]{0,1:T(8,128)(4,1)S(1)} %fusion.34, bf16[512,4,2,256]{3,0,2,1:T(8,128)(2,1)} %get-tuple-element.457, bf16[2,4096,4,256]{3,1,2,0:T(8,128)(2,1)} %get-tuple-element.456, s32[]{:T(128)S(6)} %select_n.38), kind=kOutput, calls=%fused_computation.26 | convolution fusion | flops 1080029184 | bytes 11812868 | tf_op jit(solution)/shard_map/while/body/eval_jaxpr/cond/branch_1_fun/qhgd,khd->hgqk/dot_general | solution.py:47
  197.6 1.7 fusion.21
  200.0 6.1 %multiply_add_fusion = f32[4,2,512,256]{3,2,1,0:T(8,128)} fusion(f32[4,2,512,256]{3,2,1,0:T(8,128)} %get-tuple-element.459, f32[4,2,512]{2,1,0:T(2,128)S(1)} %bitcast.69, f32[4,512,512,2]{2,1,3,0:T(8,128)S(1)} %get-tuple-element.549, f32[4,2,512]{2,1,0:T(2,128)S(1)} %max.4, pred[512,512]{0,1:T(8,128)(4,1)S(1)} %fusion.34, ...), kind=kOutput, calls=%fused_computation.32 | convolution fusion | flops 1084227584 | bytes 18120712 | tf_op jit(solution)/shard_map/while/body/eval_jaxpr/cond/branch_1_fun/hgqk,khd->hgqd/dot_general | solution.py:68
  207.4 14.5 %conditional.5 = ((f32[4,2,512]{2,1,0:T(2,128)}, f32[4,2,512]{2,1,0:T(2,128)S(1)}, f32[4,2,512,256]{3,2,1,0:T(8,128)})) conditional(s32[]{:T(128)} %convert_element_type.48, (f32[4,2,512]{2,1,0:T(2,128)}, f32[4,2,512]{2,1,0:T(2,128)S(1)}, f32[4,2,512,256]{3,2,1,0:T(8,128)}) %tuple.88, (s32[]{:T(128)}, s32[]{:T(128)}, s32[512]{0:T(512)S(1)}, ...), branch_computations={%region_6.6_spmd, %region_7.9_spmd} | conditional | flops 2174495232 | bytes 39076968 | solution.py:76
  208.5 3.5 %fusion.17 = (f32[4,2,512]{2,1,0:T(2,128)S(1)}, f32[4,512,512,2]{2,1,3,0:T(8,128)S(1)}) fusion(pred[512,512]{0,1:T(8,128)(4,1)S(1)} %fusion.34, bf16[512,4,2,256]{3,0,2,1:T(8,128)(2,1)} %get-tuple-element.457, bf16[2,4096,4,256]{3,1,2,0:T(8,128)(2,1)} %get-tuple-element.456, s32[]{:T(128)S(6)} %select_n.38), kind=kOutput, calls=%fused_computation.26 | convolution fusion | flops 1080029184 | bytes 11812868 | tf_op jit(solution)/shard_map/while/body/eval_jaxpr/cond/branch_1_fun/qhgd,khd->hgqk/dot_general | solution.py:47
  212.7 1.7 fusion.21
  215.2 6.1 %multiply_add_fusion = f32[4,2,512,256]{3,2,1,0:T(8,128)} fusion(f32[4,2,512,256]{3,2,1,0:T(8,128)} %get-tuple-element.459, f32[4,2,512]{2,1,0:T(2,128)S(1)} %bitcast.69, f32[4,512,512,2]{2,1,3,0:T(8,128)S(1)} %get-tuple-element.549, f32[4,2,512]{2,1,0:T(2,128)S(1)} %max.4, pred[512,512]{0,1:T(8,128)(4,1)S(1)} %fusion.34, ...), kind=kOutput, calls=%fused_computation.32 | convolution fusion | flops 1084227584 | bytes 18120712 | tf_op jit(solution)/shard_map/while/body/eval_jaxpr/cond/branch_1_fun/hgqk,khd->hgqd/dot_general | solution.py:68
  221.9 2.6 %select_convert_fusion = bf16[4,2,512,256]{3,2,1,0:T(8,128)(2,1)S(1)} fusion(f32[4,2,512,256]{3,2,1,0:T(8,128)} %get-tuple-element.483, f32[4,2,512]{2,1,0:T(2,128)S(1)} %broadcast_select_fusion, pred[512]{0:T(512)(128)(4,1)S(1)} %broadcast_compare_fusion.5), kind=kLoop, calls=%fused_computation.57 | loop fusion | flops 3145728 | bytes 6308352 | tf_op jit(solution)/shard_map/convert_element_type | solution.py:99
  224.5 2.5 %copy.15 = bf16[512,8,256]{2,1,0:T(8,128)(2,1)} copy(bf16[512,8,256]{2,0,1:T(8,128)(2,1)S(1)} %bitcast.66) | data formatting | bytes 4194304 | tf_op jit(solution)/shard_map/convert_element_type | solution.py:99
  (64 shorter events, 25.0 us)
Async XLA Ops:
  6.5 94.1 %all-gather.2.cloned.1.call-start = ((), (), s32[]{:S(2)}) async-start(), calls=%async_computation | async-start | bytes 18874368 | tf_op jit(solution)/shard_map/all_gather | solution.py:86
Sparse Core Ops, SparseCore 0:
  10.0 90.5 all-gather.1
where the time goes:
time: 236 us; the launch traced here: 234 us
  matrix products  81.8 us (35%)
  waiting for transfers between devices  54.7 us (23%)
  other arithmetic  41.9 us (18%)
  blocking collectives  23 us (10%)
  between operations  14.1 us (6%)
  local copies, waits for them, and re-layouts  12.5 us (5%)
  loops' own time  5.89 us (2%)
    all_gather x1, waiting for transfers between devices, shards(): shard_piece = lax.all_gather(own_pair, 'seq', axis=1, tiled=True)  54.7 us
    dot_general x9, matrix products, compute(): jnp.einsum('hgqk,khd->hgqd', weights.astype(jnp.bfloat16), kv_block[1], p...  51.9 us
    dot_general x9, matrix products, compute(): jnp.einsum('qhgd,khd->hgqk', grouped, kv_block[0], preferred_element_type...  29.9 us
    psum x1, blocking collectives, spread(): return lax.psum(kept, axis)  23 us
    reduce_sum x9, other arithmetic, compute(): totals = totals * rescale + jnp.sum(weights, axis=-1)  14.7 us
    add x9, other arithmetic, compute(): totals = totals * rescale + jnp.sum(weights, axis=-1)  6.6 us
    lt x9, other arithmetic, compute(): visible = visible & (query_pos[:, None] < length_now)  5.88 us
    max x8, other arithmetic, compute(): newest = jnp.maximum(maximum, jnp.max(masked, axis=-1))  5.86 us
  transfers between devices with their start and end apart: 1, of which 1 were waited for; matrix products, arithmetic and copies ran while one was open for 5% of the time, Pallas kernels for 0%

commit v1 on v0

--- a/solution.py
+++ b/solution.py
@@ -10,7 +10,7 @@
 
 def spread(value, axis, source):
     kept = jnp.where(lax.axis_index(axis) == source, value, 0).astype(value.dtype)
-    return lax.psum(kept, axis)
+    return jnp.sum(lax.all_gather(kept, axis), axis=0)
 
 
 def shards(queries, key_heads, projected_value_heads, lengths):

time: 236 us -> 247 us (1.047)
  waiting for transfers between devices: 54.7 us -> 70.6 us
  blocking collectives: 23 us -> 8.74 us
  local copies, waits for them, and re-layouts: 12.5 us -> 24.8 us
  matrix products: 81.8 us -> 75 us
  other arithmetic: 41.9 us -> 45.7 us
    psum x1 -> x0, blocking collectives: 23 us -> none  [spread(): return lax.psum(kept, axis)]
    all_gather x1, waiting for transfers between devices: 54.7 us -> 70.6 us  [shards(): shard_piece = lax.all_gather(own_pair, 'seq', axis=1, tiled=True)]
    unnamed x1 -> x4, local copies, waits for them, and re-layouts: 3.34 us -> 17.3 us
    all_gather x0 -> x1, blocking collectives: none -> 8.74 us  [spread(): return jnp.sum(lax.all_gather(kept, axis), axis=0)]
    dot_general x9, matrix products: 29.9 us -> 22.7 us  [compute(): jnp.einsum('qhgd,khd->hgqk', grouped, kv_block[0], preferred_element_type...]
    another operation x1, other arithmetic: 1.5 us -> 4.43 us  [shards(): own_pair = jnp.stack([key_heads, projected_value_heads])]
  transfers between devices with their start and end apart: 1 -> 1, of which waited for: 1 -> 1; matrix products, arithmetic and copies ran while one was open for 5% -> 4% of each run, Pallas kernels for 0% -> 0%
where the time goes in v1:
time: 247 us; the launch traced here: 245 us
  matrix products  75 us (30%)
  waiting for transfers between devices  70.6 us (29%)
  other arithmetic  45.7 us (19%)
  local copies, waits for them, and re-layouts  24.8 us (10%)
  between operations  14.2 us (6%)
  blocking collectives  8.74 us (4%)
  loops' own time  5.89 us (2%)
    all_gather x1, waiting for transfers between devices, shards(): shard_piece = lax.all_gather(own_pair, 'seq', axis=1, tiled=True)  70.6 us
    dot_general x9, matrix products, compute(): jnp.einsum('hgqk,khd->hgqd', weights.astype(jnp.bfloat16), kv_block[1], p...  52.3 us
    dot_general x9, matrix products, compute(): jnp.einsum('qhgd,khd->hgqk', grouped, kv_block[0], preferred_element_type...  22.7 us
    unnamed x4, local copies, waits for them, and re-layouts  17.3 us
    reduce_sum x9, other arithmetic, compute(): totals = totals * rescale + jnp.sum(weights, axis=-1)  14.7 us
    all_gather x1, blocking collectives, spread(): return jnp.sum(lax.all_gather(kept, axis), axis=0)  8.74 us
    add x9, other arithmetic, compute(): totals = totals * rescale + jnp.sum(weights, axis=-1)  6.6 us
    lt x9, other arithmetic, compute(): visible = visible & (query_pos[:, None] < length_now)  5.89 us
  transfers between devices with their start and end apart: 1, of which 1 were waited for; matrix products, arithmetic and copies ran while one was open for 4% of the time, Pallas kernels for 0%

profile of v1, /device:TPU:7, one launch (start us, length us, event | category | flops | bytes accessed | tf_op | source)
XLA Modules:
  0.0 244.9 jit_solution(16590603010850322827)
XLA Ops:
  6.5 4.4 %pad_maximum_fusion = bf16[2,512,4,256]{3,2,1,0:T(4,128)(2,1)} fusion(bf16[1,512,4,256]{3,2,1,0:T(4,128)(2,1)} %bitcast.68, bf16[1,512,4,256]{3,2,1,0:T(4,128)(2,1)} %bitcast.70), kind=kLoop, calls=%fused_computation.57 | loop fusion | flops 1048576 | bytes 4194304 | tf_op jit(solution)/shard_map/stack | solution.py:83
  11.7 2.0 copy.14
  14.5 8.7 %all-gather = bf16[16,4,4,256]{3,2,1,0:T(4,128)(2,1)S(1)} all-gather(bf16[2,4,4,256]{3,2,1,0:T(4,128)(2,1)S(1)} %fusion.36), channel_id=2, replica_groups=mesh['batch'=4,'seq'=8] {'seq'}, dimensions={0}, use_global_device_ids=true | all-gather | bytes 147456 | tf_op jit(solution)/shard_map/all_gather | solution.py:13
  23.2 7.7 %conditional.2 = (f32[4,2,512]{2,1,0:T(2,128)}, f32[4,2,512]{2,1,0:T(2,128)S(1)}, f32[4,2,512,256]{3,2,1,0:T(8,128)}) conditional(s32[]{:T(128)} %convert_element_type.37, () %tuple.61, (s32[512]{0:T(512)S(1)}, s32[4]{0:T(128)S(1)}, s32[]{:T(128)}, s32[4]{0:T(128)S(1)}, bf16[8,2,4,4,256]{4,3,2,1,0:T(4,128)(2,1)S(1)}, ...), branch_computations={%region_0.1_spmd, %region_1.5_spmd} | conditional | flops 18055684 | bytes 6878282 | solution.py:76
  26.1 0.8 fusion.4
  26.9 0.7 fusion.12
  27.6 3.3 %convolution_add_fusion = f32[4,2,512,256]{3,2,1,0:T(8,128)} fusion(f32[4,2,512]{2,1,0:T(2,128)S(1)} %get-tuple-element.557, f32[4,2,512,4]{2,3,1,0:T(4,128)S(1)} %get-tuple-element.568, f32[4,2,512]{2,1,0:T(2,128)} %get-tuple-element.656, pred[512,4]{0,1:T(4,128)(4,1)S(1)} %fusion.10, bf16[1,4,4,256]{3,2,1,0:T(4,128)(2,1)S(1)} %get-tuple-element.565), kind=kOutput, calls=%fused_computation.1 | convolution fusion | flops 9486336 | bytes 4302848 | tf_op jit(solution)/shard_map/cond/branch_1_fun/hgqk,khd->hgqd/dot_general | solution.py:68
  30.9 70.6 %all-gather.3.cloned.1.call-done = bf16[2,4096,4,256]{3,2,1,0:T(4,128)(2,1)} async-done(((bf16[2,512,4,256]{3,2,1,0:T(4,128)(2,1)}), bf16[2,4096,4,256]{3,2,1,0:T(4,128)(2,1)}) %all-gather.3.cloned.1.call-update) | async-done | bytes 16777232 | tf_op jit(solution)/shard_map/all_gather | solution.py:86
  101.5 15.3 %copy.15 = bf16[2,4096,4,256]{3,1,2,0:T(8,128)(2,1)} copy(bf16[2,4096,4,256]{3,2,1,0:T(4,128)(2,1)} %all-gather.3.cloned.1.call-done) | data formatting | bytes 33554432
  116.9 116.0 %while.22 = (s32[]{:T(128)}, f32[4,2,512]{2,1,0:T(2,128)}, f32[4,2,512]{2,1,0:T(2,128)S(1)}, f32[4,2,512,256]{3,2,1,0:T(8,128)}, s32[]{:T(128)}, /*index=5*/s32[...) while((s32[]{:T(128)}, f32[4,2,512]{2,1,0:T(2,128)}, ...), condition=%wide.region_10.11_spmd.clone, body=%wide.region_5.10_spmd.clone.sunk | while | flops 2174495232 | bytes 39079348 | solution.py:94
  117.5 13.8 %conditional.5 = ((f32[4,2,512]{2,1,0:T(2,128)}, f32[4,2,512]{2,1,0:T(2,128)S(1)}, f32[4,2,512,256]{3,2,1,0:T(8,128)})) conditional(s32[]{:T(128)} %convert_element_type.50, (f32[4,2,512]{2,1,0:T(2,128)}, f32[4,2,512]{2,1,0:T(2,128)S(1)}, f32[4,2,512,256]{3,2,1,0:T(8,128)}) %tuple.90, (s32[]{:T(128)}, s32[]{:T(128)}, s32[512]{0:T(512)S(1)}, ...), branch_computations={%region_6.6_spmd, %region_7.9_spmd} | conditional | flops 2174495232 | bytes 39076968 | solution.py:76
  118.7 2.8 %fusion.13 = (f32[4,2,512]{2,1,0:T(2,128)S(1)}, f32[4,512,512,2]{2,1,3,0:T(8,128)S(1)}) fusion(pred[512,512]{0,1:T(8,128)(4,1)S(1)} %fusion.30, bf16[512,4,2,256]{3,0,2,1:T(8,128)(2,1)S(1)} %get-tuple-element.459, bf16[2,4096,4,256]{3,1,2,0:T(8,128)(2,1)} %get-tuple-element.458, s32[]{:T(128)S(6)} %select_n.38), kind=kOutput, calls=%fused_computation.24 | convolution fusion | flops 1080029184 | bytes 11812868 | tf_op jit(solution)/shard_map/while/body/eval_jaxpr/cond/branch_1_fun/qhgd,khd->hgqk/dot_general | solution.py:47
  121.4 0.7 max.4
  122.2 1.7 fusion.17
  124.6 6.1 %multiply_add_fusion = f32[4,2,512,256]{3,2,1,0:T(8,128)} fusion(f32[4,2,512,256]{3,2,1,0:T(8,128)} %get-tuple-element.461, f32[4,2,512]{2,1,0:T(2,128)S(1)} %bitcast.72, f32[4,512,512,2]{2,1,3,0:T(8,128)S(1)} %get-tuple-element.570, f32[4,2,512]{2,1,0:T(2,128)S(1)} %max.4, pred[512,512]{0,1:T(8,128)(4,1)S(1)} %fusion.30, ...), kind=kOutput, calls=%fused_computation.30 | convolution fusion | flops 1084227584 | bytes 18120712 | tf_op jit(solution)/shard_map/while/body/eval_jaxpr/cond/branch_1_fun/hgqk,khd->hgqd/dot_general | solution.py:68
  132.0 13.8 %conditional.5 = ((f32[4,2,512]{2,1,0:T(2,128)}, f32[4,2,512]{2,1,0:T(2,128)S(1)}, f32[4,2,512,256]{3,2,1,0:T(8,128)})) conditional(s32[]{:T(128)} %convert_element_type.50, (f32[4,2,512]{2,1,0:T(2,128)}, f32[4,2,512]{2,1,0:T(2,128)S(1)}, f32[4,2,512,256]{3,2,1,0:T(8,128)}) %tuple.90, (s32[]{:T(128)}, s32[]{:T(128)}, s32[512]{0:T(512)S(1)}, ...), branch_computations={%region_6.6_spmd, %region_7.9_spmd} | conditional | flops 2174495232 | bytes 39076968 | solution.py:76
  133.2 2.8 %fusion.13 = (f32[4,2,512]{2,1,0:T(2,128)S(1)}, f32[4,512,512,2]{2,1,3,0:T(8,128)S(1)}) fusion(pred[512,512]{0,1:T(8,128)(4,1)S(1)} %fusion.30, bf16[512,4,2,256]{3,0,2,1:T(8,128)(2,1)S(1)} %get-tuple-element.459, bf16[2,4096,4,256]{3,1,2,0:T(8,128)(2,1)} %get-tuple-element.458, s32[]{:T(128)S(6)} %select_n.38), kind=kOutput, calls=%fused_computation.24 | convolution fusion | flops 1080029184 | bytes 11812868 | tf_op jit(solution)/shard_map/while/body/eval_jaxpr/cond/branch_1_fun/qhgd,khd->hgqk/dot_general | solution.py:47
  135.9 0.7 max.4
  136.7 1.7 fusion.17
  139.1 6.1 %multiply_add_fusion = f32[4,2,512,256]{3,2,1,0:T(8,128)} fusion(f32[4,2,512,256]{3,2,1,0:T(8,128)} %get-tuple-element.461, f32[4,2,512]{2,1,0:T(2,128)S(1)} %bitcast.72, f32[4,512,512,2]{2,1,3,0:T(8,128)S(1)} %get-tuple-element.570, f32[4,2,512]{2,1,0:T(2,128)S(1)} %max.4, pred[512,512]{0,1:T(8,128)(4,1)S(1)} %fusion.30, ...), kind=kOutput, calls=%fused_computation.30 | convolution fusion | flops 1084227584 | bytes 18120712 | tf_op jit(solution)/shard_map/while/body/eval_jaxpr/cond/branch_1_fun/hgqk,khd->hgqd/dot_general | solution.py:68
  146.5 13.8 %conditional.5 = ((f32[4,2,512]{2,1,0:T(2,128)}, f32[4,2,512]{2,1,0:T(2,128)S(1)}, f32[4,2,512,256]{3,2,1,0:T(8,128)})) conditional(s32[]{:T(128)} %convert_element_type.50, (f32[4,2,512]{2,1,0:T(2,128)}, f32[4,2,512]{2,1,0:T(2,128)S(1)}, f32[4,2,512,256]{3,2,1,0:T(8,128)}) %tuple.90, (s32[]{:T(128)}, s32[]{:T(128)}, s32[512]{0:T(512)S(1)}, ...), branch_computations={%region_6.6_spmd, %region_7.9_spmd} | conditional | flops 2174495232 | bytes 39076968 | solution.py:76
  147.7 2.8 %fusion.13 = (f32[4,2,512]{2,1,0:T(2,128)S(1)}, f32[4,512,512,2]{2,1,3,0:T(8,128)S(1)}) fusion(pred[512,512]{0,1:T(8,128)(4,1)S(1)} %fusion.30, bf16[512,4,2,256]{3,0,2,1:T(8,128)(2,1)S(1)} %get-tuple-element.459, bf16[2,4096,4,256]{3,1,2,0:T(8,128)(2,1)} %get-tuple-element.458, s32[]{:T(128)S(6)} %select_n.38), kind=kOutput, calls=%fused_computation.24 | convolution fusion | flops 1080029184 | bytes 11812868 | tf_op jit(solution)/shard_map/while/body/eval_jaxpr/cond/branch_1_fun/qhgd,khd->hgqk/dot_general | solution.py:47
  150.4 0.7 max.4
  151.2 1.7 fusion.17
  153.6 6.1 %multiply_add_fusion = f32[4,2,512,256]{3,2,1,0:T(8,128)} fusion(f32[4,2,512,256]{3,2,1,0:T(8,128)} %get-tuple-element.461, f32[4,2,512]{2,1,0:T(2,128)S(1)} %bitcast.72, f32[4,512,512,2]{2,1,3,0:T(8,128)S(1)} %get-tuple-element.570, f32[4,2,512]{2,1,0:T(2,128)S(1)} %max.4, pred[512,512]{0,1:T(8,128)(4,1)S(1)} %fusion.30, ...), kind=kOutput, calls=%fused_computation.30 | convolution fusion | flops 1084227584 | bytes 18120712 | tf_op jit(solution)/shard_map/while/body/eval_jaxpr/cond/branch_1_fun/hgqk,khd->hgqd/dot_general | solution.py:68
  161.1 13.8 %conditional.5 = ((f32[4,2,512]{2,1,0:T(2,128)}, f32[4,2,512]{2,1,0:T(2,128)S(1)}, f32[4,2,512,256]{3,2,1,0:T(8,128)})) conditional(s32[]{:T(128)} %convert_element_type.50, (f32[4,2,512]{2,1,0:T(2,128)}, f32[4,2,512]{2,1,0:T(2,128)S(1)}, f32[4,2,512,256]{3,2,1,0:T(8,128)}) %tuple.90, (s32[]{:T(128)}, s32[]{:T(128)}, s32[512]{0:T(512)S(1)}, ...), branch_computations={%region_6.6_spmd, %region_7.9_spmd} | conditional | flops 2174495232 | bytes 39076968 | solution.py:76
  162.2 2.8 %fusion.13 = (f32[4,2,512]{2,1,0:T(2,128)S(1)}, f32[4,512,512,2]{2,1,3,0:T(8,128)S(1)}) fusion(pred[512,512]{0,1:T(8,128)(4,1)S(1)} %fusion.30, bf16[512,4,2,256]{3,0,2,1:T(8,128)(2,1)S(1)} %get-tuple-element.459, bf16[2,4096,4,256]{3,1,2,0:T(8,128)(2,1)} %get-tuple-element.458, s32[]{:T(128)S(6)} %select_n.38), kind=kOutput, calls=%fused_computation.24 | convolution fusion | flops 1080029184 | bytes 11812868 | tf_op jit(solution)/shard_map/while/body/eval_jaxpr/cond/branch_1_fun/qhgd,khd->hgqk/dot_general | solution.py:47
  164.9 0.7 max.4
  165.7 1.7 fusion.17
  168.1 6.1 %multiply_add_fusion = f32[4,2,512,256]{3,2,1,0:T(8,128)} fusion(f32[4,2,512,256]{3,2,1,0:T(8,128)} %get-tuple-element.461, f32[4,2,512]{2,1,0:T(2,128)S(1)} %bitcast.72, f32[4,512,512,2]{2,1,3,0:T(8,128)S(1)} %get-tuple-element.570, f32[4,2,512]{2,1,0:T(2,128)S(1)} %max.4, pred[512,512]{0,1:T(8,128)(4,1)S(1)} %fusion.30, ...), kind=kOutput, calls=%fused_computation.30 | convolution fusion | flops 1084227584 | bytes 18120712 | tf_op jit(solution)/shard_map/while/body/eval_jaxpr/cond/branch_1_fun/hgqk,khd->hgqd/dot_general | solution.py:68
  175.6 13.8 %conditional.5 = ((f32[4,2,512]{2,1,0:T(2,128)}, f32[4,2,512]{2,1,0:T(2,128)S(1)}, f32[4,2,512,256]{3,2,1,0:T(8,128)})) conditional(s32[]{:T(128)} %convert_element_type.50, (f32[4,2,512]{2,1,0:T(2,128)}, f32[4,2,512]{2,1,0:T(2,128)S(1)}, f32[4,2,512,256]{3,2,1,0:T(8,128)}) %tuple.90, (s32[]{:T(128)}, s32[]{:T(128)}, s32[512]{0:T(512)S(1)}, ...), branch_computations={%region_6.6_spmd, %region_7.9_spmd} | conditional | flops 2174495232 | bytes 39076968 | solution.py:76
  176.7 2.8 %fusion.13 = (f32[4,2,512]{2,1,0:T(2,128)S(1)}, f32[4,512,512,2]{2,1,3,0:T(8,128)S(1)}) fusion(pred[512,512]{0,1:T(8,128)(4,1)S(1)} %fusion.30, bf16[512,4,2,256]{3,0,2,1:T(8,128)(2,1)S(1)} %get-tuple-element.459, bf16[2,4096,4,256]{3,1,2,0:T(8,128)(2,1)} %get-tuple-element.458, s32[]{:T(128)S(6)} %select_n.38), kind=kOutput, calls=%fused_computation.24 | convolution fusion | flops 1080029184 | bytes 11812868 | tf_op jit(solution)/shard_map/while/body/eval_jaxpr/cond/branch_1_fun/qhgd,khd->hgqk/dot_general | solution.py:47
  180.2 1.7 fusion.17
  182.7 6.1 %multiply_add_fusion = f32[4,2,512,256]{3,2,1,0:T(8,128)} fusion(f32[4,2,512,256]{3,2,1,0:T(8,128)} %get-tuple-element.461, f32[4,2,512]{2,1,0:T(2,128)S(1)} %bitcast.72, f32[4,512,512,2]{2,1,3,0:T(8,128)S(1)} %get-tuple-element.570, f32[4,2,512]{2,1,0:T(2,128)S(1)} %max.4, pred[512,512]{0,1:T(8,128)(4,1)S(1)} %fusion.30, ...), kind=kOutput, calls=%fused_computation.30 | convolution fusion | flops 1084227584 | bytes 18120712 | tf_op jit(solution)/shard_map/while/body/eval_jaxpr/cond/branch_1_fun/hgqk,khd->hgqd/dot_general | solution.py:68
  190.1 13.8 %conditional.5 = ((f32[4,2,512]{2,1,0:T(2,128)}, f32[4,2,512]{2,1,0:T(2,128)S(1)}, f32[4,2,512,256]{3,2,1,0:T(8,128)})) conditional(s32[]{:T(128)} %convert_element_type.50, (f32[4,2,512]{2,1,0:T(2,128)}, f32[4,2,512]{2,1,0:T(2,128)S(1)}, f32[4,2,512,256]{3,2,1,0:T(8,128)}) %tuple.90, (s32[]{:T(128)}, s32[]{:T(128)}, s32[512]{0:T(512)S(1)}, ...), branch_computations={%region_6.6_spmd, %region_7.9_spmd} | conditional | flops 2174495232 | bytes 39076968 | solution.py:76
  191.2 2.8 %fusion.13 = (f32[4,2,512]{2,1,0:T(2,128)S(1)}, f32[4,512,512,2]{2,1,3,0:T(8,128)S(1)}) fusion(pred[512,512]{0,1:T(8,128)(4,1)S(1)} %fusion.30, bf16[512,4,2,256]{3,0,2,1:T(8,128)(2,1)S(1)} %get-tuple-element.459, bf16[2,4096,4,256]{3,1,2,0:T(8,128)(2,1)} %get-tuple-element.458, s32[]{:T(128)S(6)} %select_n.38), kind=kOutput, calls=%fused_computation.24 | convolution fusion | flops 1080029184 | bytes 11812868 | tf_op jit(solution)/shard_map/while/body/eval_jaxpr/cond/branch_1_fun/qhgd,khd->hgqk/dot_general | solution.py:47
  194.7 1.7 fusion.17
  197.2 6.1 %multiply_add_fusion = f32[4,2,512,256]{3,2,1,0:T(8,128)} fusion(f32[4,2,512,256]{3,2,1,0:T(8,128)} %get-tuple-element.461, f32[4,2,512]{2,1,0:T(2,128)S(1)} %bitcast.72, f32[4,512,512,2]{2,1,3,0:T(8,128)S(1)} %get-tuple-element.570, f32[4,2,512]{2,1,0:T(2,128)S(1)} %max.4, pred[512,512]{0,1:T(8,128)(4,1)S(1)} %fusion.30, ...), kind=kOutput, calls=%fused_computation.30 | convolution fusion | flops 1084227584 | bytes 18120712 | tf_op jit(solution)/shard_map/while/body/eval_jaxpr/cond/branch_1_fun/hgqk,khd->hgqd/dot_general | solution.py:68
  204.6 13.8 %conditional.5 = ((f32[4,2,512]{2,1,0:T(2,128)}, f32[4,2,512]{2,1,0:T(2,128)S(1)}, f32[4,2,512,256]{3,2,1,0:T(8,128)})) conditional(s32[]{:T(128)} %convert_element_type.50, (f32[4,2,512]{2,1,0:T(2,128)}, f32[4,2,512]{2,1,0:T(2,128)S(1)}, f32[4,2,512,256]{3,2,1,0:T(8,128)}) %tuple.90, (s32[]{:T(128)}, s32[]{:T(128)}, s32[512]{0:T(512)S(1)}, ...), branch_computations={%region_6.6_spmd, %region_7.9_spmd} | conditional | flops 2174495232 | bytes 39076968 | solution.py:76
  205.7 2.8 %fusion.13 = (f32[4,2,512]{2,1,0:T(2,128)S(1)}, f32[4,512,512,2]{2,1,3,0:T(8,128)S(1)}) fusion(pred[512,512]{0,1:T(8,128)(4,1)S(1)} %fusion.30, bf16[512,4,2,256]{3,0,2,1:T(8,128)(2,1)S(1)} %get-tuple-element.459, bf16[2,4096,4,256]{3,1,2,0:T(8,128)(2,1)} %get-tuple-element.458, s32[]{:T(128)S(6)} %select_n.38), kind=kOutput, calls=%fused_computation.24 | convolution fusion | flops 1080029184 | bytes 11812868 | tf_op jit(solution)/shard_map/while/body/eval_jaxpr/cond/branch_1_fun/qhgd,khd->hgqk/dot_general | solution.py:47
  209.2 1.7 fusion.17
  211.7 6.1 %multiply_add_fusion = f32[4,2,512,256]{3,2,1,0:T(8,128)} fusion(f32[4,2,512,256]{3,2,1,0:T(8,128)} %get-tuple-element.461, f32[4,2,512]{2,1,0:T(2,128)S(1)} %bitcast.72, f32[4,512,512,2]{2,1,3,0:T(8,128)S(1)} %get-tuple-element.570, f32[4,2,512]{2,1,0:T(2,128)S(1)} %max.4, pred[512,512]{0,1:T(8,128)(4,1)S(1)} %fusion.30, ...), kind=kOutput, calls=%fused_computation.30 | convolution fusion | flops 1084227584 | bytes 18120712 | tf_op jit(solution)/shard_map/while/body/eval_jaxpr/cond/branch_1_fun/hgqk,khd->hgqd/dot_general | solution.py:68
  219.1 13.8 %conditional.5 = ((f32[4,2,512]{2,1,0:T(2,128)}, f32[4,2,512]{2,1,0:T(2,128)S(1)}, f32[4,2,512,256]{3,2,1,0:T(8,128)})) conditional(s32[]{:T(128)} %convert_element_type.50, (f32[4,2,512]{2,1,0:T(2,128)}, f32[4,2,512]{2,1,0:T(2,128)S(1)}, f32[4,2,512,256]{3,2,1,0:T(8,128)}) %tuple.90, (s32[]{:T(128)}, s32[]{:T(128)}, s32[512]{0:T(512)S(1)}, ...), branch_computations={%region_6.6_spmd, %region_7.9_spmd} | conditional | flops 2174495232 | bytes 39076968 | solution.py:76
  220.2 2.8 %fusion.13 = (f32[4,2,512]{2,1,0:T(2,128)S(1)}, f32[4,512,512,2]{2,1,3,0:T(8,128)S(1)}) fusion(pred[512,512]{0,1:T(8,128)(4,1)S(1)} %fusion.30, bf16[512,4,2,256]{3,0,2,1:T(8,128)(2,1)S(1)} %get-tuple-element.459, bf16[2,4096,4,256]{3,1,2,0:T(8,128)(2,1)} %get-tuple-element.458, s32[]{:T(128)S(6)} %select_n.38), kind=kOutput, calls=%fused_computation.24 | convolution fusion | flops 1080029184 | bytes 11812868 | tf_op jit(solution)/shard_map/while/body/eval_jaxpr/cond/branch_1_fun/qhgd,khd->hgqk/dot_general | solution.py:47
  223.7 1.7 fusion.17
  226.2 6.1 %multiply_add_fusion = f32[4,2,512,256]{3,2,1,0:T(8,128)} fusion(f32[4,2,512,256]{3,2,1,0:T(8,128)} %get-tuple-element.461, f32[4,2,512]{2,1,0:T(2,128)S(1)} %bitcast.72, f32[4,512,512,2]{2,1,3,0:T(8,128)S(1)} %get-tuple-element.570, f32[4,2,512]{2,1,0:T(2,128)S(1)} %max.4, pred[512,512]{0,1:T(8,128)(4,1)S(1)} %fusion.30, ...), kind=kOutput, calls=%fused_computation.30 | convolution fusion | flops 1084227584 | bytes 18120712 | tf_op jit(solution)/shard_map/while/body/eval_jaxpr/cond/branch_1_fun/hgqk,khd->hgqd/dot_general | solution.py:68
  232.9 2.6 %select_convert_fusion = bf16[4,2,512,256]{3,2,1,0:T(8,128)(2,1)S(1)} fusion(f32[4,2,512,256]{3,2,1,0:T(8,128)} %get-tuple-element.485, f32[4,2,512]{2,1,0:T(2,128)S(1)} %broadcast_select_fusion, pred[512]{0:T(512)(128)(4,1)S(1)} %broadcast_compare_fusion.5), kind=kLoop, calls=%fused_computation.55 | loop fusion | flops 3145728 | bytes 6308352 | tf_op jit(solution)/shard_map/convert_element_type | solution.py:99
  235.6 2.5 %copy.22 = bf16[512,8,256]{2,1,0:T(8,128)(2,1)} copy(bf16[512,8,256]{2,0,1:T(8,128)(2,1)S(1)} %bitcast.65) | data formatting | bytes 4194304 | tf_op jit(solution)/shard_map/convert_element_type | solution.py:99
  (68 shorter events, 26.0 us)
Async XLA Ops:
  6.5 95.0 %all-gather.3.cloned.1.call-start = ((), (), s32[]{:S(2)}) async-start(), calls=%async_computation | async-start | bytes 18874368 | tf_op jit(solution)/shard_map/all_gather | solution.py:86
  11.0 2.8 %copy-start = (bf16[512,4,256]{2,1,0:T(4,128)(2,1)S(1)}, bf16[512,4,256]{2,1,0:T(4,128)(2,1)}, u32[]{:S(2)}) copy-start(bf16[512,4,256]{2,1,0:T(4,128)(2,1)} %param.12) | copy-start | bytes 3145732
Sparse Core Ops, SparseCore 0:
  11.1 90.3 all-gather.2
